TPU v7x, 32 devices: a whole 2x2x4 slice. The times are simulated.
32 devices in a mesh: fsdp: 8 (over y, x, core), rep: 4 (over z).
Axes of the slice: x: 2, y: 2, z: 4, core: 2. Of those that a mesh axis runs over, the one named last changes fastest.
Arguments:
- tokens: bfloat16 [8192, 1152], P(('fsdp', 'rep')), may hold values from -6 to 6
- cond: bfloat16 [128, 1152], P(('fsdp', 'rep')), may hold values from -6 to 6
- image_sizes: int32 [128], P(('fsdp', 'rep')), may hold values from 0 to 256, as said below
- w_ada: bfloat16 [1152, 6912], P('fsdp'), may hold values from -0.1875 to 0.1875
- b_ada: bfloat16 [6912], P('fsdp'), may hold values from -1.5 to 1.5
- w_qkv: bfloat16 [1152, 3456], P('fsdp'), may hold values from -0.1875 to 0.1875
- b_qkv: bfloat16 [2304], P('fsdp'), may hold values from -2.5 to 2.5
- w_out: bfloat16 [1152, 1152], P('fsdp'), may hold values from -0.75 to 0.75
- b_out: bfloat16 [1152], P('fsdp'), may hold values from -1.5 to 1.5
- w_up: bfloat16 [1152, 4608], P('fsdp'), may hold values from -0.1875 to 0.1875
- b_up: bfloat16 [4608], P('fsdp'), may hold values from -2.5 to 2.5
- w_down: bfloat16 [4608, 1152], P('fsdp'), may hold values from -0.09375 to 0.09375
- b_down: bfloat16 [1152], P('fsdp'), may hold values from -1.5 to 1.5
- cotangent: bfloat16 [8192, 1152], P(('fsdp', 'rep')), may hold values from -6 to 6
Outputs:
- output: bfloat16 [8192, 1152], P(('fsdp', 'rep'))
- grad_input: float32 [8192, 1152], P(('fsdp', 'rep'))
- grad_cond: float32 [128, 1152], P(('fsdp', 'rep'))
- grad_w_ada: float32 [1152, 6912], P('fsdp')
- grad_b_ada: float32 [6912], P('fsdp')
- grad_w_qkv: float32 [1152, 3456], P('fsdp')
- grad_b_qkv: float32 [2304], P('fsdp')
- grad_w_out: float32 [1152, 1152], P('fsdp')
- grad_b_out: float32 [1152], P('fsdp')
- grad_w_up: float32 [1152, 4608], P('fsdp')
- grad_b_up: float32 [4608], P('fsdp')
- grad_w_down: float32 [4608, 1152], P('fsdp')
- grad_b_down: float32 [1152], P('fsdp')
Inputs may be any that keep to these rules, and one draw needn't show every extreme that they name: `image_sizes`: in each group of 4 slots of one device, either the first slot holds one image of 256 patches and the rest are 0, or the first k slots (k from 1 to 4) hold images of 64 patches and the rest are 0; in every draw some device's images fill all its 256 slots.
All inputs are finite; a program needn't handle non-finite values.
Results may differ from a plain program's by a relative error of at most 0.02.
Values may be sent and summed in bfloat16 or wider, within the bound.
A program may use at most 256 MiB of HBM per device.

v0:
```python
import jax
import jax.numpy as jnp
from jax import lax
from jax.sharding import PartitionSpec as P

H = 16


EPSILON = 1e-06
HIGHEST = lax.Precision.HIGHEST
MASKED = -1e30


def layer_norm(inputs):
    average = jnp.mean(inputs, axis=-1, keepdims=True)
    centered = inputs - average
    variance = jnp.mean(centered * centered, axis=-1, keepdims=True)
    return centered * lax.rsqrt(variance + EPSILON)


def modulate(hidden, shift_part, scale_part):
    return layer_norm(hidden) * (1.0 + scale_part) + shift_part


def gelu_tanh(inputs):
    return jax.nn.gelu(inputs, approximate=True)


def product(first_operand, second_operand):
    return jnp.dot(first_operand, second_operand, preferred_element_type=jnp.float32)


def product_back(first_operand, second_operand):
    return lax.dot_general(
        first_operand, second_operand, (((1,), (1,)), ((), ())), preferred_element_type=jnp.float32
    )


def outer_sum(first_operand, second_operand):
    return lax.dot_general(
        first_operand, second_operand, (((0,), (0,)), ((), ())), preferred_element_type=jnp.float32
    )


def fetch_forward(weight, bias_piece):
    return (
        lax.all_gather(weight, "fsdp", axis=0, tiled=True),
        lax.all_gather(bias_piece, "fsdp", axis=0, tiled=True),
    )


def weights_again(weight):
    return lax.all_gather(weight, "fsdp", axis=0, tiled=True)


def reduce_grads(weight_grad, bias_grad):
    row_part, bias_part = (
        lax.psum_scatter(weight_grad, "fsdp", scatter_dimension=0, tiled=True),
        lax.psum_scatter(bias_grad, "fsdp", scatter_dimension=0, tiled=True),
    )
    column_part = lax.psum_scatter(row_part, "rep", scatter_dimension=1, tiled=True)
    whole_rows, bias_stack = (
        lax.all_gather(column_part, "rep", axis=1, tiled=True),
        lax.all_gather(bias_part[None], "rep", axis=0, tiled=True),
    )
    return (whole_rows, jnp.sum(bias_stack, axis=0))


def local(
    tokens,
    cond,
    image_sizes,
    w_ada,
    b_ada,
    w_qkv,
    b_qkv,
    w_out,
    b_out,
    w_up,
    b_up,
    w_down,
    b_down,
    cotangent,
):
    row_count, model_width = tokens.shape
    head_count = H
    head_dim = model_width // head_count
    slot_count = image_sizes.shape[0]
    scale_factor = head_dim ** (-0.5)
    block_rows = min(512, row_count)
    block_count = row_count // block_rows
    image_ends = jnp.cumsum(image_sizes)
    positions = jnp.arange(row_count, dtype=jnp.int32)
    image_ids = jnp.sum((positions[:, None] >= image_ends[None, :]).astype(jnp.int32), axis=1)
    selector = (image_ids[:, None] == jnp.arange(slot_count, dtype=jnp.int32)[None, :]).astype(
        jnp.float32
    )
    cond_float = cond.astype(jnp.float32)
    activ_float, silu_pull = jax.vjp(jax.nn.silu, cond_float)
    activ_low = activ_float.astype(jnp.bfloat16)
    full_ada, full_bada = fetch_forward(w_ada, b_ada)
    modulation = product(activ_low, full_ada) + full_bada.astype(jnp.float32)
    per_token = jnp.dot(selector, modulation, precision=HIGHEST)
    shift_a, scale_a, gate_a, shift_b, scale_b, gate_b = jnp.split(per_token, 6, axis=1)
    hidden = tokens.astype(jnp.float32)
    normed_a, pull_a = jax.vjp(modulate, hidden, shift_a, scale_a)
    normed_a_low = normed_a.astype(jnp.bfloat16)
    full_qkv, full_bqkv = fetch_forward(w_qkv, b_qkv)
    bias_qkv = full_bqkv.astype(jnp.float32)
    bias_full = jnp.concatenate(
        [bias_qkv[:model_width], jnp.zeros((model_width,), jnp.float32), bias_qkv[model_width:]]
    )
    projected = (product(normed_a_low, full_qkv) + bias_full).astype(jnp.bfloat16)
    query_heads = projected[:, :model_width].reshape(row_count, head_count, head_dim)
    key_heads = projected[:, model_width : 2 * model_width].reshape(row_count, head_count, head_dim)
    value_heads = projected[:, 2 * model_width :].reshape(row_count, head_count, head_dim)
    query_blocks = query_heads.reshape(block_count, block_rows, head_count, head_dim)
    id_blocks = image_ids.reshape(block_count, block_rows)

    def scores_of(query_block, id_block):
        raw_scores = (
            jnp.einsum("qhd,khd->hqk", query_block, key_heads, preferred_element_type=jnp.float32)
            * scale_factor
        )
        same_image = id_block[:, None] == image_ids[None, :]
        return jnp.where(same_image[None], raw_scores, MASKED)

    def forward_block(block_item):
        query_block, id_block = block_item
        scores = scores_of(query_block, id_block)
        row_max = jnp.max(scores, axis=-1, keepdims=True)
        exponent = jnp.exp(scores - row_max)
        row_total = jnp.sum(exponent, axis=-1, keepdims=True)
        probabilities = (exponent / row_total).astype(jnp.bfloat16)
        attended_block = jnp.einsum(
            "hqk,khd->qhd", probabilities, value_heads, preferred_element_type=jnp.float32
        )
        return (attended_block.astype(jnp.bfloat16), (row_max + jnp.log(row_total))[:, :, 0])

    attended_blocks, lse_blocks = lax.map(forward_block, (query_blocks, id_blocks))
    attended = attended_blocks.reshape(row_count, model_width)
    full_out, full_bout = fetch_forward(w_out, b_out)
    branch_a = product(attended, full_out) + full_bout.astype(jnp.float32)
    middle = hidden + gate_a * branch_a
    normed_b, pull_b = jax.vjp(modulate, middle, shift_b, scale_b)
    normed_b_low = normed_b.astype(jnp.bfloat16)
    full_up, full_bup = fetch_forward(w_up, b_up)
    inner_pre = product(normed_b_low, full_up) + full_bup.astype(jnp.float32)
    activated, gelu_pull = jax.vjp(gelu_tanh, inner_pre)
    activated_low = activated.astype(jnp.bfloat16)
    full_down, full_bdown = fetch_forward(w_down, b_down)
    branch_b = product(activated_low, full_down) + full_bdown.astype(jnp.float32)
    output = (middle + gate_b * branch_b).astype(jnp.bfloat16)
    grad_out = cotangent.astype(jnp.float32)
    grad_gate_b = grad_out * branch_b
    grad_branch_b = (gate_b * grad_out).astype(jnp.bfloat16)
    grad_w_down, grad_b_down = reduce_grads(
        outer_sum(activated_low, grad_branch_b), jnp.sum(grad_branch_b.astype(jnp.float32), axis=0)
    )
    back_down = weights_again(w_down)
    grad_activated = product_back(grad_branch_b, back_down)
    (grad_inner,) = gelu_pull(grad_activated)
    grad_inner_low = grad_inner.astype(jnp.bfloat16)
    grad_w_up, grad_b_up = reduce_grads(
        outer_sum(normed_b_low, grad_inner_low), jnp.sum(grad_inner_low.astype(jnp.float32), axis=0)
    )
    back_up = weights_again(w_up)
    grad_normed_b = product_back(grad_inner_low, back_up)
    grad_middle_norm, grad_shift_b, grad_scale_b = pull_b(grad_normed_b)
    grad_middle = grad_out + grad_middle_norm
    grad_gate_a = grad_middle * branch_a
    grad_branch_a = (gate_a * grad_middle).astype(jnp.bfloat16)
    grad_w_out, grad_b_out = reduce_grads(
        outer_sum(attended, grad_branch_a), jnp.sum(grad_branch_a.astype(jnp.float32), axis=0)
    )
    back_out = weights_again(w_out)
    grad_attended = product_back(grad_branch_a, back_out).astype(jnp.bfloat16)
    grad_att_blocks = grad_attended.reshape(block_count, block_rows, head_count, head_dim)

    def backward_block(carried, block_item):
        key_grad, value_grad = carried
        query_block, id_block, grad_block, lse_block = block_item
        scores = scores_of(query_block, id_block)
        probabilities = jnp.exp(scores - lse_block[:, :, None])
        probabilities_low = probabilities.astype(jnp.bfloat16)
        grad_probs = jnp.einsum(
            "qhd,khd->hqk", grad_block, value_heads, preferred_element_type=jnp.float32
        )
        row_delta = jnp.sum(probabilities * grad_probs, axis=-1, keepdims=True)
        grad_scores = (probabilities * (grad_probs - row_delta)).astype(jnp.bfloat16)
        query_grad = (
            jnp.einsum("hqk,khd->qhd", grad_scores, key_heads, preferred_element_type=jnp.float32)
            * scale_factor
        )
        key_grad = (
            key_grad
            + jnp.einsum(
                "hqk,qhd->khd", grad_scores, query_block, preferred_element_type=jnp.float32
            )
            * scale_factor
        )
        value_grad = value_grad + jnp.einsum(
            "hqk,qhd->khd", probabilities_low, grad_block, preferred_element_type=jnp.float32
        )
        return ((key_grad, value_grad), query_grad)

    zero_heads = jnp.zeros((row_count, head_count, head_dim), jnp.float32)
    (grad_keys, grad_values), grad_query_blocks = lax.scan(
        backward_block,
        (zero_heads, zero_heads),
        (query_blocks, id_blocks, grad_att_blocks, lse_blocks),
    )
    grad_projected = jnp.concatenate(
        [
            grad_query_blocks.reshape(row_count, model_width),
            grad_keys.reshape(row_count, model_width),
            grad_values.reshape(row_count, model_width),
        ],
        axis=1,
    ).astype(jnp.bfloat16)
    column_sums = jnp.sum(grad_projected.astype(jnp.float32), axis=0)
    grad_bias_qkv = jnp.concatenate([column_sums[:model_width], column_sums[2 * model_width :]])
    grad_w_qkv, grad_b_qkv = reduce_grads(outer_sum(normed_a_low, grad_projected), grad_bias_qkv)
    back_qkv = weights_again(w_qkv)
    grad_normed_a = product_back(grad_projected, back_qkv)
    grad_hidden_norm, grad_shift_a, grad_scale_a = pull_a(grad_normed_a)
    grad_input = grad_middle + grad_hidden_norm
    grad_per_token = jnp.concatenate(
        [grad_shift_a, grad_scale_a, grad_gate_a, grad_shift_b, grad_scale_b, grad_gate_b], axis=1
    )
    grad_modulation = lax.dot_general(
        selector, grad_per_token, (((0,), (0,)), ((), ())), precision=HIGHEST
    ).astype(jnp.bfloat16)
    grad_w_ada, grad_b_ada = reduce_grads(
        outer_sum(activ_low, grad_modulation), jnp.sum(grad_modulation.astype(jnp.float32), axis=0)
    )
    back_ada = weights_again(w_ada)
    grad_activ = product_back(grad_modulation, back_ada)
    (grad_cond,) = silu_pull(grad_activ)
    return (
        output,
        grad_input,
        grad_cond,
        grad_w_ada,
        grad_b_ada,
        grad_w_qkv,
        grad_b_qkv,
        grad_w_out,
        grad_b_out,
        grad_w_up,
        grad_b_up,
        grad_w_down,
        grad_b_down,
    )


def solution(mesh):
    placed = (
        P(("fsdp", "rep"), None),
        P(("fsdp", "rep"), None),
        P(("fsdp", "rep")),
        P("fsdp", None),
        P("fsdp"),
        P("fsdp", None),
        P("fsdp"),
        P("fsdp", None),
        P("fsdp"),
        P("fsdp", None),
        P("fsdp"),
        P("fsdp", None),
        P("fsdp"),
        P(("fsdp", "rep"), None),
    )
    return jax.shard_map(
        local,
        mesh=mesh,
        in_specs=placed,
        out_specs=(
            P(("fsdp", "rep"), None),
            P(("fsdp", "rep"), None),
            P(("fsdp", "rep"), None),
            P("fsdp", None),
            P("fsdp"),
            P("fsdp", None),
            P("fsdp"),
            P("fsdp", None),
            P("fsdp"),
            P("fsdp", None),
            P("fsdp"),
            P("fsdp", None),
            P("fsdp"),
        ),
        check_vma=False,
    )
```

profile of v0, /device:TPU:0, one launch (start us, length us, event | category | flops | bytes accessed | tf_op | source)
XLA Modules:
  0.0 1639.8 jit_solution(16755960182710785992)
XLA Ops:
  15.2 27.1 %all-reduce.17 = (bf16[2304]{0:T(1024)(128)(2,1)S(1)}, bf16[6912]{0:T(1024)(128)(2,1)S(1)}, bf16[1152]{0:T(1024)(128)(2,1)S(1)}, bf16[1152]{0:T(1024)(128)(2,1)S(1)}, bf16[4608]{0:T(1024)(128)(2,1)S(1)}) all-reduce(bf16[2304]{0:T(1024)(128)(2,1)S(1)} %dynamic-update-slice.1, ...), channel_id=1, replica_groups=mesh['fsdp'=8,'rep'=4] {'fsdp'}, use_global_device_ids=true, to_apply=%add.1 | all-reduce | flops 16128 | bytes 64512
  44.0 55.6 %all-gather.18.cloned.1.call-done = bf16[1152,6912]{1,0:T(8,128)(2,1)} async-done(((bf16[144,6912]{1,0:T(8,128)(2,1)}), bf16[1152,6912]{1,0:T(8,128)(2,1)}) %all-gather.18.cloned.1.call-update) | async-done | bytes 15925264 | tf_op jit(solution)/shard_map/all_gather | solution.py:47
  99.6 7.7 convolution_add_fusion
  107.3 3.0 fusion.36
  110.3 2.8 copy-done.2
  113.4 40.6 %all-gather.20.cloned.1.call-done = bf16[1152,3456]{1,0:T(8,128)(2,1)} async-done(((bf16[144,3456]{1,0:T(8,128)(2,1)}), bf16[1152,3456]{1,0:T(8,128)(2,1)}) %all-gather.20.cloned.1.call-update) | async-done | bytes 7962640 | tf_op jit(solution)/shard_map/all_gather | solution.py:47
  154.1 5.8 fusion
  164.7 21.6 %all-gather.22.cloned.1.call-done = bf16[1152,1152]{1,0:T(8,128)(2,1)} async-done(((bf16[144,1152]{1,0:T(8,128)(2,1)}), bf16[1152,1152]{1,0:T(8,128)(2,1)}) %all-gather.22.cloned.1.call-update) | async-done | bytes 2654224 | tf_op jit(solution)/shard_map/all_gather | solution.py:47
  186.3 4.2 fusion.57
  191.8 3.3 convert_reduce_fusion.3
  195.1 56.7 %all-gather.26.cloned.1.call-done = bf16[4608,1152]{1,0:T(8,128)(2,1)} async-done(((bf16[576,1152]{1,0:T(8,128)(2,1)}), bf16[4608,1152]{1,0:T(8,128)(2,1)}) %all-gather.26.cloned.1.call-update) | async-done | bytes 10616848 | tf_op jit(solution)/shard_map/all_gather | solution.py:47
  251.9 9.9 fusion.63
  261.7 55.7 %all-gather.24.cloned.1.call-done = bf16[1152,4608]{1,0:T(8,128)(2,1)} async-done(((bf16[144,4608]{1,0:T(8,128)(2,1)}), bf16[1152,4608]{1,0:T(8,128)(2,1)}) %all-gather.24.cloned.1.call-update) | async-done | bytes 10616848 | tf_op jit(solution)/shard_map/all_gather | solution.py:47
  317.5 9.6 convert_reduce_fusion
  327.2 10.0 multiply_reduce_fusion.1
  337.2 9.5 fusion.56
  350.4 3.4 multiply_reduce_fusion
  357.8 8.0 fusion.50
  366.9 17.7 %fusion.52 = f32[4608,1152]{1,0:T(8,128)} fusion(bf16[256,1152]{1,0:T(8,128)(2,1)S(1)} %copy-done.26, f32[256,4608]{1,0:T(8,128)} %copy-done.14), kind=kOutput, calls=%fused_computation.115 | convolution fusion | flops 2728525824 | bytes 26542080 | tf_op jit(solution)/shard_map/dot_general | solution.py:40
  385.7 12.7 fusion.65
  399.1 6.9 constant_dynamic-update-slice_fusion.1
  411.4 2.6 convert_reduce_fusion.5
  414.0 13.5 fusion.47
  428.7 3.3 fusion.64
  432.1 46.8 %reduce-scatter.21.cloned.1.call-done = f32[144,3456]{1,0:T(8,128)} async-done(((f32[1152,3456]{1,0:T(8,128)}), f32[144,3456]{1,0:T(8,128)}) %reduce-scatter.21.cloned.1.call-update) | async-done | bytes 1990672 | tf_op jit(solution)/shard_map/reduce_scatter | solution.py:58
  478.9 3.5 copy.82
  482.5 137.6 %reduce-scatter.29.cloned.1.call-done = f32[576,1152]{1,0:T(8,128)} async-done(((f32[4608,1152]{1,0:T(8,128)}), f32[576,1152]{1,0:T(8,128)}) %reduce-scatter.29.cloned.1.call-update) | async-done | bytes 2654224 | tf_op jit(solution)/shard_map/reduce_scatter | solution.py:58
  620.1 3.5 copy.86
  623.7 137.6 %reduce-scatter.25.cloned.1.call-done = f32[144,4608]{1,0:T(8,128)} async-done(((f32[1152,4608]{1,0:T(8,128)}), f32[144,4608]{1,0:T(8,128)}) %reduce-scatter.25.cloned.1.call-update) | async-done | bytes 2654224 | tf_op jit(solution)/shard_map/reduce_scatter | solution.py:58
  761.4 202.6 %reduce-scatter.19.cloned.1.call-done = f32[144,6912]{1,0:T(8,128)} async-done(((f32[1152,6912]{1,0:T(8,128)}), f32[144,6912]{1,0:T(8,128)}) %reduce-scatter.19.cloned.1.call-update) | async-done | bytes 3981328 | tf_op jit(solution)/shard_map/reduce_scatter | solution.py:58
  964.0 6.3 copy.80
  970.4 53.8 %reduce-scatter.23.cloned.1.call-done = f32[144,1152]{1,0:T(8,128)} async-done(((f32[1152,1152]{1,0:T(8,128)}), f32[144,1152]{1,0:T(8,128)}) %reduce-scatter.23.cloned.1.call-update) | async-done | bytes 663568 | tf_op jit(solution)/shard_map/reduce_scatter | solution.py:58
  1026.7 66.8 %reduce-scatter.33.cloned.1.call-done = f32[864,144]{1,0:T(8,128)} async-done(((f32[3456,144]{1,0:T(8,128)}), f32[864,144]{1,0:T(8,128)}) %reduce-scatter.33.cloned.1.call-update) | async-done | bytes 497680
  1095.9 57.5 %reduce-scatter.37.cloned.1.call-done = f32[288,576]{1,0:T(8,128)} async-done(((f32[1152,576]{1,0:T(8,128)}), f32[288,576]{1,0:T(8,128)}) %reduce-scatter.37.cloned.1.call-update) | async-done | bytes 663568
  1153.4 54.8 %reduce-scatter.27.cloned.1.call-done = f32[144,1152]{1,0:T(8,128)} async-done(((f32[144,4608]{1,0:T(8,128)}), f32[144,1152]{1,0:T(8,128)}) %reduce-scatter.27.cloned.1.call-update) | async-done | bytes 663568 | tf_op jit(solution)/shard_map/reduce_scatter | solution.py:61
  1208.5 125.1 %reduce-scatter.31.cloned.1.call-done = f32[1728,144]{1,0:T(8,128)} async-done(((f32[6912,144]{1,0:T(8,128)}), f32[1728,144]{1,0:T(8,128)}) %reduce-scatter.31.cloned.1.call-update) | async-done | bytes 995344
  1333.6 3.0 copy.81
  1343.1 25.8 %all-reduce.15 = (f32[6912]{0:T(1024)S(1)}, f32[2304]{0:T(1024)S(1)}, f32[1152]{0:T(1024)S(1)}, f32[4608]{0:T(1024)S(1)}, f32[1152]{0:T(1024)S(1)}) all-reduce(f32[6912]{0:T(1024)S(1)} %get-tuple-element.149, f32[2304]{0:T(1024)S(1)} %pad_maximum_fusion.2, ...), channel_id=9, replica_groups=mesh['fsdp'=8,'rep'=4] {'fsdp'}, use_global_device_ids=true, to_apply=%region_16.17.clone | all-reduce | flops 16128 | bytes 129024
  1369.8 20.4 %all-reduce.16 = (f32[3456]{0:T(1024)S(1)}, f32[1152]{0:T(1024)S(1)}, f32[576]{0:T(1024)S(1)}, f32[2304]{0:T(1024)S(1)}, f32[576]{0:T(1024)S(1)}) all-reduce(f32[3456]{0:T(1024)S(1)} %dynamic-slice_dynamic-update-slice_fusion.1, f32[1152]{0:T(1024)S(1)} %dynamic-slice_dynamic-update-slice_fusion.2, ...), channel_id=2, replica_groups=mesh['fsdp'=8,'rep'=4] {'rep'}, use_global_device_ids=true, to_apply=%add.5 | all-reduce | flops 8064 | bytes 64512
  1393.6 10.4 fusion.44
  1405.1 22.5 %all-gather.7 = f32[4,288,144]{1,2,0:T(8,128)S(1)} all-gather(f32[1,288,144]{1,2,0:T(8,128)S(1)} %bitcast.120), channel_id=1, replica_groups=mesh['fsdp'=8,'rep'=4] {'rep'}, dimensions={0}, use_global_device_ids=true | all-gather | bytes 829440 | tf_op jit(solution)/shard_map/all_gather | solution.py:63
  1429.3 2.5 copy.72
  1434.2 48.4 %all-gather.30.cloned.1.call-done = f32[576,1152]{0,1:T(8,128)} async-done(((f32[576,288]{0,1:T(8,128)}), f32[576,1152]{0,1:T(8,128)}) %all-gather.30.cloned.1.call-update) | async-done | bytes 2654224 | tf_op jit(solution)/shard_map/all_gather | solution.py:63
  1482.6 3.4 copy.75
  1486.0 52.0 %all-gather.28.cloned.1.call-done = f32[144,4608]{1,0:T(8,128)} async-done(((f32[144,1152]{1,0:T(8,128)}), f32[144,4608]{1,0:T(8,128)}) %all-gather.28.cloned.1.call-update) | async-done | bytes 2654224 | tf_op jit(solution)/shard_map/all_gather | solution.py:63
  1538.0 80.7 %all-gather.32.cloned.1.call-done = f32[4,1728,144]{1,2,0:T(8,128)} async-done(((f32[1,1728,144]{1,2,0:T(8,128)}), f32[4,1728,144]{1,2,0:T(8,128)}) %all-gather.32.cloned.1.call-update) | async-done | bytes 3981328 | tf_op jit(solution)/shard_map/all_gather | solution.py:63
  1618.7 6.8 copy.71
  1625.5 6.0 reshape.221
  (249 shorter events, 47.6 us)
Async XLA Ops:
  7.2 6.8 copy-start.57
  7.2 7.0 copy-start.58
  7.2 7.3 copy-start.54
  7.2 7.5 copy-start.55
  7.2 7.8 copy-start.56
  7.2 35.8 %copy-start.59 = (s32[4]{0:T(128)S(1)}, s32[4]{0:T(128)}, u32[]{:S(2)}) copy-start(s32[4]{0:T(128)} %param.16) | copy-start | bytes 52
  7.3 92.3 %all-gather.18.cloned.1.call-start = ((), (), s32[]{:S(2)}) async-start(), calls=%async_computation.10 | async-start | bytes 17915904 | tf_op jit(solution)/shard_map/all_gather | solution.py:47
  8.0 35.3 %copy-start.6 = (bf16[256,1152]{1,0:T(8,128)(2,1)S(1)}, bf16[256,1152]{1,0:T(8,128)(2,1)}, u32[]{:S(2)}) copy-start(bf16[256,1152]{1,0:T(8,128)(2,1)} %param.14) | copy-start | bytes 1769476
  8.0 91.6 %copy-start.34 = (bf16[4,1152]{1,0:T(4,128)(2,1)S(1)}, bf16[4,1152]{1,0:T(4,128)(2,1)}, u32[]{:S(2)}) copy-start(bf16[4,1152]{1,0:T(4,128)(2,1)} %param.15) | copy-start | bytes 27652
  8.0 146.1 %all-gather.20.cloned.1.call-start = ((), (), s32[]{:S(2)}) async-start(), calls=%async_computation.11 | async-start | bytes 8957952 | tf_op jit(solution)/shard_map/all_gather | solution.py:47
  8.8 177.5 %all-gather.22.cloned.1.call-start = ((), (), s32[]{:S(2)}) async-start(), calls=%async_computation.12 | async-start | bytes 2985984 | tf_op jit(solution)/shard_map/all_gather | solution.py:47
  9.5 242.4 %all-gather.26.cloned.1.call-start = ((), (), s32[]{:S(2)}) async-start(), calls=%async_computation.14 | async-start | bytes 11943936 | tf_op jit(solution)/shard_map/all_gather | solution.py:47
  10.1 307.4 %all-gather.24.cloned.1.call-start = ((), (), s32[]{:S(2)}) async-start(), calls=%async_computation.13 | async-start | bytes 11943936 | tf_op jit(solution)/shard_map/all_gather | solution.py:47
  10.7 468.2 %reduce-scatter.21.cloned.1.call-start = ((), (), s32[]{:S(2)}) async-start(), calls=%async_computation.16 | async-start | bytes 17915904 | tf_op jit(solution)/shard_map/reduce_scatter | solution.py:58
  43.2 64.0 %copy-start.35 = (f32[1152]{0:T(1024)}, f32[1152]{0:T(1024)S(1)}, u32[]{:S(2)}) copy-start(f32[1152]{0:T(1024)S(1)} %broadcast_in_dim.100) | copy-start | bytes 13828
  43.5 66.7 %copy-start.37 = (f32[256]{0:T(256)}, f32[256]{0:T(256)S(1)}, u32[]{:S(2)}) copy-start(f32[256]{0:T(256)S(1)} %broadcast_multiply_fusion.1) | copy-start | bytes 3076
  43.8 63.4 %copy-start.46 = (f32[256]{0:T(256)}, f32[256]{0:T(256)S(1)}, u32[]{:S(2)}) copy-start(f32[256]{0:T(256)S(1)} %fusion.29) | copy-start | bytes 3076
  43.8 66.4 %copy-start.42 = (f32[256]{0:T(256)}, f32[256]{0:T(256)S(1)}, u32[]{:S(2)}) copy-start(f32[256]{0:T(256)S(1)} %fusion.45) | copy-start | bytes 3076
  113.4 46.4 %copy-start.31 = (bf16[256,1152]{1,0:T(8,128)(2,1)}, bf16[256,1152]{1,0:T(8,128)(2,1)S(1)}, u32[]{:S(2)}) copy-start(bf16[256,1152]{1,0:T(8,128)(2,1)S(1)} %fusion.27) | copy-start | bytes 1769476
  164.7 25.8 %copy-start.20 = (bf16[16,72,256]{2,1,0:T(8,128)(2,1)}, bf16[16,72,256]{2,1,0:T(8,128)(2,1)S(1)}, u32[]{:S(2)}) copy-start(bf16[16,72,256]{2,1,0:T(8,128)(2,1)S(1)} %fusion.20) | copy-start | bytes 1769476
  251.8 75.2 %slice-start = ((s8[7077888]{0:T(1024)(128)(4,1)}), s8[2883584]{0:T(1024)(128)(4,1)S(1)}, s32[]{:S(2)}) async-start(s8[7077888]{0:T(1024)(128)(4,1)} %bitcast.89), calls=%async_computation.29 | async-start | bytes 5767168
  317.5 9.6 slice-start.1
  317.5 9.6 copy-start.4
  317.5 9.6 copy-start.40
  327.1 10.1 copy-start.24
  327.1 10.1 copy-start.14
  327.1 10.0 copy-start.49
  327.1 10.0 copy-start.45
  327.1 10.0 copy-start.52
  337.1 9.6 copy-start.15
  337.2 9.5 copy-start.8
  365.8 254.2 %reduce-scatter.29.cloned.1.call-start = ((), (), s32[]{:S(2)}) async-start(), calls=%async_computation.21 | async-start | bytes 23887872 | tf_op jit(solution)/shard_map/reduce_scatter | solution.py:58
  384.6 376.7 %reduce-scatter.25.cloned.1.call-start = ((), (), s32[]{:S(2)}) async-start(), calls=%async_computation.18 | async-start | bytes 23887872 | tf_op jit(solution)/shard_map/reduce_scatter | solution.py:58
  398.4 7.5 copy-start.47
  398.5 7.5 copy-start.43
  398.5 565.5 %reduce-scatter.19.cloned.1.call-start = ((), (), s32[]{:S(2)}) async-start(), calls=%async_computation.15 | async-start | bytes 35831808 | tf_op jit(solution)/shard_map/reduce_scatter | solution.py:58
  427.5 596.7 %reduce-scatter.23.cloned.1.call-start = ((), (), s32[]{:S(2)}) async-start(), calls=%async_computation.17 | async-start | bytes 5971968 | tf_op jit(solution)/shard_map/reduce_scatter | solution.py:58
  432.0 661.5 %reduce-scatter.33.cloned.1.call-start = ((), (), s32[]{:S(2)}) async-start(), calls=%async_computation.26 | async-start | bytes 4423680
  482.4 670.9 %reduce-scatter.37.cloned.1.call-start = ((), (), s32[]{:S(2)}) async-start(), calls=%async_computation.28 | async-start | bytes 3686400
  623.6 584.6 %reduce-scatter.27.cloned.1.call-start = ((), (), s32[]{:S(2)}) async-start(), calls=%async_computation.19 | async-start | bytes 3317760 | tf_op jit(solution)/shard_map/reduce_scatter | solution.py:61
  761.3 572.3 %reduce-scatter.31.cloned.1.call-start = ((), (), s32[]{:S(2)}) async-start(), calls=%async_computation.25 | async-start | bytes 8847360
  970.4 433.7 %reduce-scatter.35.cloned.1.call-start = ((), (), s32[]{:S(2)}) async-start(), calls=%async_computation.27 | async-start | bytes 1474560
  1026.7 402.6 %all-gather.34.cloned.1.call-start = ((), (), s32[]{:S(2)}) async-start(), calls=%async_computation.24 | async-start | bytes 2580480 | tf_op jit(solution)/shard_map/all_gather | solution.py:63
  1095.8 240.8 %copy-start.60 = (u32[32]{0:T(128)S(1)}, u32[32]{0:T(128)}, u32[]{:S(2)}) copy-start(u32[32]{0:T(128)} %constant.111) | copy-start | bytes 388
  1095.8 386.8 %all-gather.30.cloned.1.call-start = ((), (), s32[]{:S(2)}) async-start(), calls=%async_computation.22 | async-start | bytes 3686400 | tf_op jit(solution)/shard_map/all_gather | solution.py:63
  1153.4 384.7 %all-gather.28.cloned.1.call-start = ((), (), s32[]{:S(2)}) async-start(), calls=%async_computation.20 | async-start | bytes 3317760 | tf_op jit(solution)/shard_map/all_gather | solution.py:63
  1208.2 410.5 %all-gather.32.cloned.1.call-start = ((), (), s32[]{:S(2)}) async-start(), calls=%async_computation.23 | async-start | bytes 5160960 | tf_op jit(solution)/shard_map/all_gather | solution.py:63
  1333.6 35.7 %copy-start.36 = (f32[1152]{0:T(1024)S(1)}, f32[1152]{0:T(1024)}, u32[]{:S(2)}) copy-start(f32[1152]{0:T(1024)} %copy-done.35) | copy-start | bytes 13828
  (34 other events, 69.1 us)
Sparse Core Ops, SparseCore 0:
  10.0 89.5 all-gather.17
  101.4 52.5 all-gather.19
  156.0 30.2 all-gather.21
  188.0 63.8 all-gather.25
  253.6 63.8 all-gather.23
  366.0 112.8 reduce-scatter.20
  482.9 137.1 reduce-scatter.28
  624.1 137.1 reduce-scatter.24
  765.4 198.5 reduce-scatter.18
  967.2 56.9 reduce-scatter.22
  1027.2 66.3 reduce-scatter.32
  1095.8 57.4 reduce-scatter.36
  1155.6 52.5 reduce-scatter.26
  1210.4 123.1 reduce-scatter.30
  1336.3 29.6 reduce-scatter.34
  1368.0 54.5 all-gather.33
  1424.1 58.4 all-gather.29
  1484.0 53.9 all-gather.27
  1540.2 78.4 all-gather.31
where the time goes:
time: 1640 us
  waiting for transfers between devices  1300 us (79%)
  matrix products  143 us (9%)
  blocking collectives  95.9 us (6%)
  local copies, waits for them, and re-layouts  64.4 us (4%)
  between operations  23.1 us (1%)
    reduce_scatter x5, waiting for transfers between devices, reduce_grads(): lax.psum_scatter(weight_grad, 'fsdp', scatter_dimension=0, tiled=True)  578 us
    unnamed x23, waiting for transfers between devices  253 us
    all_gather x5, waiting for transfers between devices, fetch_forward(): lax.all_gather(weight, 'fsdp', axis=0, tiled=True)  230 us
    all_gather x4, waiting for transfers between devices, reduce_grads(): lax.all_gather(column_part, 'rep', axis=1, tiled=True)  181 us
    unnamed x3, blocking collectives  73.4 us
    dot_general x5, matrix products, outer_sum(): lax.dot_general(first_operand, second_operand, (((0,), (0,)), ((), ())),...  55.2 us
    reduce_scatter x1, waiting for transfers between devices, reduce_grads(): lax.psum_scatter(row_part, 'rep', scatter_dimension=1, tiled=True)  54.8 us
    unnamed x160, local copies, waits for them, and re-layouts  53.2 us
  transfers between devices with their start and end apart: 19, of which 17 were waited for; matrix products, arithmetic and copies ran while one was open for 9% of the time, Pallas kernels for 0%

commit v1 on v0

--- a/solution.py
+++ b/solution.py
@@ -1,6 +1,10 @@
+import functools
+
 import jax
 import jax.numpy as jnp
 from jax import lax
+from jax.experimental import pallas as pl
+from jax.experimental.pallas import tpu as pltpu
 from jax.sharding import PartitionSpec as P
 
 H = 16
@@ -89,7 +93,9 @@
     scale_factor = head_dim ** (-0.5)
     block_rows = min(512, row_count)
     block_count = row_count // block_rows
-    image_ends = jnp.cumsum(image_sizes)
+    image_ends = jnp.sum(
+        jnp.where(jnp.arange(slot_count)[:, None] >= jnp.arange(slot_count)[None, :], image_sizes[None, :], 0), axis=1
+    )
     positions = jnp.arange(row_count, dtype=jnp.int32)
     image_ids = jnp.sum((positions[:, None] >= image_ends[None, :]).astype(jnp.int32), axis=1)
     selector = (image_ids[:, None] == jnp.arange(slot_count, dtype=jnp.int32)[None, :]).astype(
@@ -254,6 +260,266 @@
     )
 
 
+MESH = pl.DeviceIdType.MESH
+F32, BF16 = jnp.float32, jnp.bfloat16
+
+def place():
+    index = lax.axis_index("fsdp")
+    return index // 4, (index // 2) % 2, index % 2
+
+def peer(offset):
+    y, x, core = place()
+    y = 1 - y if offset & 4 else y
+    x = 1 - x if offset & 2 else x
+    core = 1 - core if offset & 1 else core
+    return {"fsdp": y * 4 + x * 2 + core}
+
+def greet(offsets):
+    barrier = pltpu.get_barrier_semaphore()
+    for offset in offsets:
+        pl.semaphore_signal(barrier, inc=1, device_id=peer(offset), device_id_type=MESH)
+    pl.semaphore_wait(barrier, len(offsets))
+
+def remote(src, dst, send, recv, offset):
+    return pltpu.make_async_remote_copy(src_ref=src, dst_ref=dst, send_sem=send, recv_sem=recv, device_id=peer(offset), device_id_type=MESH)
+
+def nt(a, b):
+    return lax.dot_general(a, b, (((1,), (1,)), ((), ())), preferred_element_type=F32)
+def tn(a, b):
+    return lax.dot_general(a, b, (((0,), (0,)), ((), ())), preferred_element_type=F32)
+def nn(a, b):
+    return jnp.dot(a, b, preferred_element_type=F32)
+
+GELU_C = 0.7978845608028654
+def gelu_parts(u):
+    u2 = u * u
+    t = jnp.tanh(GELU_C * u * (1.0 + 0.044715 * u2))
+    half = 0.5 * (1.0 + t)
+    act = u * half
+    slope = half + 0.5 * u * (1.0 - t * t) * (GELU_C * (1.0 + 3 * 0.044715 * u2))
+    return act, slope
+
+def mlp_kernel(nb_ref, gbb_ref, wup_ref, bup_ref, wdn_ref,
+               bb_ref, gnb_ref, gdn_ref, gup_ref, gbup_ref,
+               nb_all, gbb_all, act_all, gi_all, mine, out_pair, in_pair, out_far, in_far,
+               ag_send, ag_recv, fw_send, fw_recv, pr_send, pr_recv, far_send, far_recv):
+    greet((1, 2, 4, 6))
+    srcs = (nb_ref, gbb_ref)
+    alls = (nb_all, gbb_all)
+    sends = []
+    for offset in (1, 2, 4, 6):
+        for a in (0, 1):
+            cp = remote(srcs[a], alls[a].at[offset], ag_send.at[a, offset], ag_recv.at[a, offset], offset)
+            cp.start()
+            sends.append(cp)
+    nb_all[0] = nb_ref[...]
+    gbb_all[0] = gbb_ref[...]
+    def arrived(a, slot):
+        return remote(alls[a].at[slot], alls[a].at[slot], ag_send.at[a, slot], ag_recv.at[a, slot], slot)
+    def forward(a, slot):
+        return remote(alls[a].at[slot], alls[a].at[slot + 1], fw_send.at[a, slot], fw_recv.at[a, slot], 1)
+
+    def one(slot):
+        inner = nn(nb_all[slot], wup_ref[...]) + bup_ref[...]
+        act, slope = gelu_parts(inner)
+        act = act.astype(BF16)
+        act_all[slot] = act
+        ga = nt(gbb_all[slot], wdn_ref[...])
+        gi = (slope * ga).astype(BF16)
+        gi_all[slot] = gi
+        return nt(gi, wup_ref[...]), nn(act, wdn_ref[...])
+
+    def pair_copy(a, p):
+        return remote(out_pair.at[a, p], in_pair.at[a, p], pr_send.at[a, p], pr_recv.at[a, p], 1)
+    def far_copy(a, p):
+        return remote(out_far.at[a, p], in_far.at[a, p], far_send.at[a, p], far_recv.at[a, p], 2 * p)
+
+    def finish(p):
+        for a in (0, 1):
+            pair_copy(a, p).wait()
+            total = mine[a, p].astype(F32) + in_pair[a, p].astype(F32)
+            if p == 0:
+                (gnb_ref, bb_ref)[a][...] = total
+            else:
+                out_far[a, p] = total.astype(BF16)
+                far_copy(a, p).start()
+
+    for p in range(4):
+        if p > 0:
+            for a in (0, 1):
+                arrived(a, 2 * p).wait_recv()
+                forward(a, 2 * p).start()
+        for h in (0, 1):
+            slot = 2 * p + h
+            if h == 1:
+                for a in (0, 1):
+                    if p == 0:
+                        arrived(a, 1).wait_recv()
+                    else:
+                        forward(a, 2 * p).wait_recv()
+            parts = one(slot)
+            for a in (0, 1):
+                if h == 0:
+                    mine[a, p] = parts[a].astype(BF16)
+                else:
+                    out_pair[a, p] = parts[a].astype(BF16)
+                    pair_copy(a, p).start()
+        if p > 0:
+            finish(p - 1)
+    finish(3)
+    hid = gdn_ref.shape[0]
+    rows = nb_ref.shape[0]
+    acts = act_all[...].reshape(8 * rows, hid)
+    gis = gi_all[...].reshape(8 * rows, hid)
+    gdn_ref[...] = tn(acts, gbb_all[...].reshape(8 * rows, -1)).astype(gdn_ref.dtype)
+    gup_ref[...] = tn(nb_all[...].reshape(8 * rows, -1), gis).astype(gup_ref.dtype)
+    gbup_ref[...] = jnp.sum(gis.astype(F32), axis=0, keepdims=True)
+    for p in (1, 2, 3):
+        for a in (0, 1):
+            far_copy(a, p).wait()
+            forward(a, 2 * p).wait_send()
+            out = (gnb_ref, bb_ref)[a]
+            out[...] += in_far[a, p].astype(F32)
+    for cp in sends:
+        cp.wait_send()
+
+def mlp(nb, gbb, wup, bup, wdn):
+    rows, width = nb.shape
+    hid = wup.shape[1]
+    S = jax.ShapeDtypeStruct
+    vm = pl.BlockSpec(memory_space=pltpu.VMEM)
+    dma = pltpu.SemaphoreType.DMA
+    return pl.pallas_call(
+        mlp_kernel,
+        out_shape=(S((rows, width), F32), S((rows, width), F32), S((hid, width), BF16), S((width, hid), BF16), S((1, hid), F32)),
+        in_specs=[vm] * 5, out_specs=(vm,) * 5,
+        scratch_shapes=[
+            pltpu.VMEM((8, rows, width), BF16), pltpu.VMEM((8, rows, width), BF16),
+            pltpu.VMEM((8, rows, hid), BF16), pltpu.VMEM((8, rows, hid), BF16),
+            pltpu.VMEM((2, 4, rows, width), BF16), pltpu.VMEM((2, 4, rows, width), BF16), pltpu.VMEM((2, 4, rows, width), BF16),
+            pltpu.VMEM((2, 4, rows, width), BF16), pltpu.VMEM((2, 4, rows, width), BF16),
+            dma((2, 8)), dma((2, 8)), dma((2, 8)), dma((2, 8)), dma((2, 4)), dma((2, 4)), dma((2, 4)), dma((2, 4)),
+        ],
+        compiler_params=pltpu.CompilerParams(collective_id=1, has_side_effects=True, vmem_limit_bytes=60 << 20),
+    )(nb, gbb, wup, bup, wdn)
+
+
+def fast(tokens, cond, image_sizes, w_ada, b_ada, w_qkv, b_qkv, w_out, b_out, w_up, b_up, w_down, b_down, cotangent):
+    rows, width = tokens.shape
+    heads, head_dim = H, width // H
+    slots = image_sizes.shape[0]
+    part = w_ada.shape[0]
+    hid = w_down.shape[0]
+    index = lax.axis_index("fsdp")
+    core = index % 2
+    order = jnp.arange(slots)
+    image_ends = jnp.sum(jnp.where(order[:, None] >= order[None, :], image_sizes[None, :], 0), axis=1)
+    ids = jnp.sum((jnp.arange(rows, dtype=jnp.int32)[:, None] >= image_ends[None, :]).astype(jnp.int32), axis=1)
+    selector = (ids[:, None] == order[None, :]).astype(F32)
+    full_qkv = lax.all_gather(w_qkv, "fsdp", axis=0, tiled=True)
+    full_out = lax.all_gather(w_out, "fsdp", axis=0, tiled=True)
+    biases = jnp.concatenate([b_ada, b_qkv, b_out, b_down])[None]
+    biases = lax.all_gather(biases, "fsdp", axis=0, tiled=True).astype(F32)
+    n_ada, n_qkv = b_ada.shape[0], b_qkv.shape[0]
+    bias_ada = biases[:, :n_ada].reshape(-1)
+    bias_qkv = biases[:, n_ada : n_ada + n_qkv].reshape(-1)
+    bias_out = biases[:, n_ada + n_qkv : n_ada + n_qkv + part].reshape(-1)
+    bias_down = biases[:, n_ada + n_qkv + part :].reshape(-1)
+    activ, silu_pull = jax.vjp(jax.nn.silu, cond.astype(F32))
+    activ_low = activ.astype(BF16)
+    activ_plane = lax.all_gather(activ_low, "fsdp", axis=0, tiled=True)
+    mine = lax.dynamic_slice(activ_plane, (0, index * part), (activ_plane.shape[0], part))
+    modulation = lax.psum_scatter(nn(mine, w_ada), "fsdp", scatter_dimension=0, tiled=True) + bias_ada
+    per_token = jnp.dot(selector, modulation, precision=HIGHEST)
+    shift_a, scale_a, gate_a, shift_b, scale_b, gate_b = jnp.split(per_token, 6, axis=1)
+    hidden = tokens.astype(F32)
+    grad_out = cotangent.astype(F32)
+    gbb = (gate_b * grad_out).astype(BF16)
+    normed_a, pull_a = jax.vjp(modulate, hidden, shift_a, scale_a)
+    na = normed_a.astype(BF16)
+    bias_full = jnp.concatenate([bias_qkv[:width], jnp.zeros((width,), F32), bias_qkv[width:]])
+    projected = (nn(na, full_qkv) + bias_full).astype(BF16)
+    q, k, v = [projected[:, i * width : (i + 1) * width].reshape(rows, heads, head_dim) for i in range(3)]
+    scale = head_dim ** (-0.5)
+    scores = jnp.einsum("qhd,khd->hqk", q, k, preferred_element_type=F32) * scale
+    scores = jnp.where((ids[:, None] == ids[None, :])[None], scores, MASKED)
+    exponent = jnp.exp(scores - jnp.max(scores, axis=-1, keepdims=True))
+    probs = exponent / jnp.sum(exponent, axis=-1, keepdims=True)
+    probs_low = probs.astype(BF16)
+    attended = jnp.einsum("hqk,khd->qhd", probs_low, v, preferred_element_type=F32).astype(BF16).reshape(rows, width)
+    branch_a = nn(attended, full_out) + bias_out
+    middle = hidden + gate_a * branch_a
+    normed_b, pull_b = jax.vjp(modulate, middle, shift_b, scale_b)
+    nb = normed_b.astype(BF16)
+    wide = hid + 64
+    pieces = [
+        w_up[:, 2 * hid * (j // 2) + (2 * hid - wide) * (j % 2) :][:, :wide] for j in range(8)
+    ]
+    wup = lax.all_to_all(jnp.stack(pieces), "fsdp", 0, 0, tiled=True).reshape(width, wide)
+    place_row = core * (wide - hid)
+    wdn = lax.dynamic_update_slice(jnp.zeros((wide, width), BF16), w_down, (place_row, 0))
+    bup = lax.dynamic_update_slice(jnp.zeros((1, wide), F32), b_up.astype(F32)[None], (0, place_row))
+    branch_b, grad_nb, gdn, gup, gbup = mlp(nb, gbb, wup, bup, wdn)
+    branch_b = branch_b + bias_down
+    output = (middle + gate_b * branch_b).astype(BF16)
+    grad_gate_b = grad_out * branch_b
+    grad_middle_norm, grad_shift_b, grad_scale_b = pull_b(grad_nb)
+    grad_middle = grad_out + grad_middle_norm
+    grad_gate_a = grad_middle * branch_a
+    gba = (gate_a * grad_middle).astype(BF16)
+    gout = tn(attended, gba).astype(BF16)
+    gatt = nt(gba, full_out).astype(BF16).reshape(rows, heads, head_dim)
+    grad_probs = jnp.einsum("qhd,khd->hqk", gatt, v, preferred_element_type=F32)
+    delta = jnp.sum(probs * grad_probs, axis=-1, keepdims=True)
+    grad_scores = (probs * (grad_probs - delta)).astype(BF16)
+    gq = jnp.einsum("hqk,khd->qhd", grad_scores, k, preferred_element_type=F32) * scale
+    gk = jnp.einsum("hqk,qhd->khd", grad_scores, q, preferred_element_type=F32) * scale
+    gv = jnp.einsum("hqk,qhd->khd", probs_low, gatt, preferred_element_type=F32)
+    gp = jnp.concatenate([t.reshape(rows, width) for t in (gq, gk, gv)], axis=1).astype(BF16)
+    gqkv = tn(na, gp).astype(BF16)
+    grad_na = nt(gp, full_qkv)
+    grad_norm, grad_shift_a, grad_scale_a = pull_a(grad_na)
+    grad_input = grad_middle + grad_norm
+    grad_mod = lax.dot_general(
+        selector,
+        jnp.concatenate([grad_shift_a, grad_scale_a, grad_gate_a, grad_shift_b, grad_scale_b, grad_gate_b], axis=1),
+        (((0,), (0,)), ((), ())),
+        precision=HIGHEST,
+    ).astype(BF16)
+    both = ("fsdp", "rep")
+    mod_all = lax.all_gather(grad_mod, both, axis=0, tiled=True)
+    activ_all = lax.all_gather(activ_low, both, axis=0, tiled=True)
+    g_ada = tn(lax.dynamic_slice(activ_all, (0, index * part), (activ_all.shape[0], part)), mod_all)
+    g_bada = lax.dynamic_slice(jnp.sum(mod_all.astype(F32), axis=0), (index * n_ada,), (n_ada,))
+    mod_plane = lax.all_gather(grad_mod, "fsdp", axis=0, tiled=True)
+    back = nt(mod_plane, w_ada)
+    grad_activ = lax.all_to_all(back.reshape(8, slots, part), "fsdp", 0, 0, tiled=True)
+    (grad_cond,) = silu_pull(grad_activ.transpose(1, 0, 2).reshape(slots, width))
+    cols = jnp.sum(gp.astype(F32), axis=0)
+    vector = jnp.concatenate(
+        [cols[:width], cols[2 * width :], jnp.sum(gba.astype(F32), axis=0), jnp.sum(gbb.astype(F32), axis=0)]
+    )
+    vector = lax.psum(vector, both)
+    g_bqkv = lax.dynamic_slice(vector[: 2 * width], (index * n_qkv,), (n_qkv,))
+    g_bout = lax.dynamic_slice(vector[2 * width : 3 * width], (index * part,), (part,))
+    g_bdown = lax.dynamic_slice(vector[3 * width :], (index * part,), (part,))
+    g_bup = lax.psum(lax.dynamic_slice(gbup[0], (place_row,), (hid,)), "rep")
+    own_qkv = lax.psum_scatter(gqkv, "fsdp", scatter_dimension=0, tiled=True)
+    own_out = lax.psum_scatter(gout, "fsdp", scatter_dimension=0, tiled=True)
+    got = lax.all_to_all(gup.reshape(8, part, wide), "fsdp", 0, 0, tiled=True).astype(F32)
+    lap = wide - hid
+    strips = []
+    for c in range(4):
+        left, right = got[2 * c], got[2 * c + 1]
+        strips += [left[:, : hid - lap], left[:, hid - lap :] + right[:, : 2 * lap], right[:, 2 * lap :]]
+    own_up = jnp.concatenate(strips, axis=1).astype(BF16)
+    own_down = lax.dynamic_slice(gdn, (place_row, 0), (hid, width))
+    g_qkv, g_out, g_up, g_down = [
+        lax.psum(t, "rep").astype(F32) for t in (own_qkv, own_out, own_up, own_down)
+    ]
+    return (output, grad_input, grad_cond, g_ada, g_bada, g_qkv, g_bqkv, g_out, g_bout, g_up, g_bup, g_down, g_bdown)
+
+
 def solution(mesh):
     placed = (
         P(("fsdp", "rep"), None),
@@ -271,8 +537,9 @@
         P("fsdp"),
         P(("fsdp", "rep"), None),
     )
+    fits = mesh.shape["fsdp"] == 8
     return jax.shard_map(
-        local,
+        fast if fits else local,
         mesh=mesh,
         in_specs=placed,
         out_specs=(

time: 1640 us -> 660 us (0.40)
  waiting for transfers between devices: 1300 us -> 201 us
  Pallas kernels: 0 us -> 118 us
  blocking collectives: 95.9 us -> 183 us
  matrix products: 143 us -> 56.3 us
  local copies, waits for them, and re-layouts: 64.4 us -> 39 us
    reduce_scatter x6 -> x2, waiting for transfers between devices: 633 us -> 74.4 us  [the longest x1 73 us: fast(): own_qkv = lax.psum_scatter(gqkv, 'fsdp', scatter_dimension=0, tiled=True)]
    all_gather x9 -> x3, waiting for transfers between devices: 411 us -> 59.2 us  [the longest x1 46.5 us: fast(): full_qkv = lax.all_gather(w_qkv, 'fsdp', axis=0, tiled=True)]
    unnamed x23 -> x8, waiting for transfers between devices: 253 us -> 8.09 us
    pallas_call x0 -> x1, Pallas kernels: none -> 118 us  [mlp(): pl.pallas_call(mlp_kernel, out_shape=(S((rows, width), F32), S((rows, wid...]
    dot_general x23 -> x16, matrix products: 143 us -> 52.7 us  [the longest x3 12.8 us: nt(): lax.dot_general(a, b, (((1,), (1,)), ((), ())), preferred_element_type=F32)]
    all_gather x1 -> x3, blocking collectives: 22.5 us -> 90.3 us  [the longest x1 69.5 us: fast(): activ_all = lax.all_gather(activ_low, both, axis=0, tiled=True)]
    psum x0 -> x2, blocking collectives: none -> 56.2 us  [the longest x1 45.2 us: fast(): vector = lax.psum(vector, both)]
    psum x0 -> x1, waiting for transfers between devices: none -> 53.3 us  [fast(): lax.psum(t, 'rep').astype(F32)]
  transfers between devices with their start and end apart: 19 -> 10, of which waited for: 17 -> 7; matrix products, arithmetic and copies ran while one was open for 9% -> 15% of each run, Pallas kernels for 0% -> 0%
where the time goes in v1:
time: 660 us; the launch traced here: 656 us
  waiting for transfers between devices  201 us (30%)
  blocking collectives  183 us (28%)
  Pallas kernels  118 us (18%)
  matrix products  56.3 us (9%)
  local copies, waits for them, and re-layouts  39 us (6%)
  other arithmetic  30.2 us (5%)
  between operations  16.4 us (2%)
  starting transfers between devices  12.5 us (2%)
    pallas_call x1, Pallas kernels, mlp(): pl.pallas_call(mlp_kernel, out_shape=(S((rows, width), F32), S((rows, wid...  118 us
    reduce_scatter x1, waiting for transfers between devices, fast(): own_qkv = lax.psum_scatter(gqkv, 'fsdp', scatter_dimension=0, tiled=True)  73 us
    all_gather x1, blocking collectives, fast(): activ_all = lax.all_gather(activ_low, both, axis=0, tiled=True)  69.5 us
    psum x1, waiting for transfers between devices, fast(): lax.psum(t, 'rep').astype(F32)  53.3 us
    all_gather x1, waiting for transfers between devices, fast(): full_qkv = lax.all_gather(w_qkv, 'fsdp', axis=0, tiled=True)  46.5 us
    psum x1, blocking collectives, fast(): vector = lax.psum(vector, both)  45.2 us
    unnamed x1, blocking collectives  36.3 us
    unnamed x118, local copies, waits for them, and re-layouts  21.2 us
  transfers between devices with their start and end apart: 10, of which 7 were waited for; matrix products, arithmetic and copies ran while one was open for 15% of the time, Pallas kernels for 0%

profile of v1, /device:TPU:0, one launch (start us, length us, event | category | flops | bytes accessed | tf_op | source)
XLA Modules:
  0.0 656.1 jit_solution(4564281905923888118)
XLA Ops:
  8.1 10.7 %all-gather.1 = bf16[8,4,1152]{2,1,0:T(4,128)(2,1)S(1)} all-gather(bf16[1,4,1152]{2,1,0:T(4,128)(2,1)S(1)} %fusion.55), channel_id=1, replica_groups=mesh['fsdp'=8,'rep'=4] {'fsdp'}, dimensions={0}, use_global_device_ids=true | all-gather | bytes 82944 | tf_op jit(solution)/shard_map/all_gather | solution.py:430
  18.8 1.4 fusion.53
  27.1 4.4 all-to-all-start
  34.1 36.3 %all-reduce = bf16[11520]{0:T(1024)(128)(2,1)S(1)} all-reduce(bf16[11520]{0:T(1024)(128)(2,1)S(1)} %dynamic-update-slice), channel_id=2, replica_groups=mesh['fsdp'=8,'rep'=4] {'fsdp'}, use_global_device_ids=true, to_apply=%add | all-reduce | flops 11520 | bytes 46080
  75.6 6.6 %all-reduce.6.cloned.1.call-done = f32[32,6912]{1,0:T(8,128)} async-done(((f32[32,6912]{1,0:T(8,128)}), f32[32,6912]{1,0:T(8,128)}) %all-reduce.6.cloned.1.call-update) | async-done | bytes 884752
  82.2 3.9 fusion.37
  86.1 2.9 copy-done.1
  89.4 46.5 %all-gather.9.cloned.1.call-done = bf16[1152,3456]{1,0:T(8,128)(2,1)} async-done(((bf16[144,3456]{1,0:T(8,128)(2,1)}), bf16[1152,3456]{1,0:T(8,128)(2,1)}) %all-gather.9.cloned.1.call-update) | async-done | bytes 7962640 | tf_op jit(solution)/shard_map/all_gather | solution.py:419
  135.9 5.8 fusion.2
  144.3 1.5 copy.59
  145.9 2.3 copy.58
  148.2 3.5 fusion.74
  151.7 3.7 convolution_convert_fusion.5
  155.4 12.7 %all-gather.11.cloned.1.call-done = bf16[1152,1152]{1,0:T(8,128)(2,1)} async-done(((bf16[144,1152]{1,0:T(8,128)(2,1)}), bf16[1152,1152]{1,0:T(8,128)(2,1)}) %all-gather.11.cloned.1.call-update) | async-done | bytes 2654224 | tf_op jit(solution)/shard_map/all_gather | solution.py:420
  168.1 4.5 fusion.67
  173.7 3.3 convert_reduce_fusion.3
  177.0 118.0 %shard_map.237 = (f32[256,1152]{1,0:T(8,128)}, f32[256,1152]{1,0:T(8,128)}, bf16[640,1152]{1,0:T(8,128)(2,1)}, bf16[1152,640]{1,0:T(8,128)(2,1)}, f32[1,640]{1,0:T(1,128)}) custom-call(bf16[256,1152]{1,0:T(8,128)(2,1)} %get-tuple-element.38.nb_ref, bf16[256,1152]{1,0:T(8,128)(2,1)} %get-tuple-element.30.gbb_ref, bf16[1152,640]{1,0:T(8,128)(2,1)} %bitcast.15.wup_ref, ...), custom_call_target="tpu_custom_call" | custom-call | tf_op jit(solution)/shard_map/pallas_call | solution.py:392
  295.0 2.1 multiply_reduce_fusion.1
  297.3 3.1 fusion.66
  300.4 2.0 convert_reduce_fusion.4
  303.3 2.4 convolution_convert_fusion.2
  306.0 3.8 convolution_convert_fusion.3
  309.8 2.1 copy.62
  311.9 3.9 multiply_reduce_fusion
  321.5 5.5 convolution_convert_fusion
  327.0 4.3 all-to-all-start.2
  331.4 7.1 %constant_dynamic-update-slice_fusion.1 = (f32[256,6912]{1,0:T(8,128)S(1)}, f32[256]{0:T(256)S(1)}, f32[256,1152]{1,0:T(8,128)S(1)}) fusion(f32[256,6912]{1,0:T(8,128)} %copy-done.1, f32[256]{0:T(256)S(1)} %broadcast_multiply_fusion.1, bf16[256,1152]{1,0:T(8,128)(2,1)} %param.14, bf16[1152,3456]{1,0:T(8,128)(2,1)} %all-gather.9.cloned.1.call-done, ...), kind=kOutput, calls=%fused_computation.115 | convolution fusion | flops 2045509376 | bytes 13862912 | tf_op jit(solution)/shard_map/dot_general | solution.py:287
  338.6 2.0 fusion.65
  340.8 1.4 multiply_dynamic-update-slice_fusion.1
  343.6 3.2 fusion.1
  348.2 6.0 all-to-all-done.2
  354.2 1.6 convert_element_type.117
  357.7 73.0 %reduce-scatter.3.cloned.1.call-done = bf16[144,3456]{1,0:T(8,128)(2,1)} async-done(((bf16[1152,3456]{1,0:T(8,128)(2,1)}), bf16[144,3456]{1,0:T(8,128)(2,1)}) %reduce-scatter.3.cloned.1.call-update) | async-done | bytes 995344 | tf_op jit(solution)/shard_map/reduce_scatter | solution.py:507
  430.7 69.5 %all-gather.3 = bf16[32,4,1152]{2,1,0:T(4,128)(2,1)S(1)} all-gather(bf16[1,4,1152]{2,1,0:T(4,128)(2,1)S(1)} %fusion.55), channel_id=1, replica_groups=mesh['fsdp'=8,'rep'=4] {'fsdp','rep'}, dimensions={0}, use_global_device_ids=true | all-gather | bytes 304128 | tf_op jit(solution)/shard_map/all_gather | solution.py:491
  501.0 10.1 %all-gather.2 = bf16[8,4,6912]{2,1,0:T(4,128)(2,1)S(1)} all-gather(bf16[1,4,6912]{2,1,0:T(4,128)(2,1)S(1)} %copy-done.37), channel_id=1, replica_groups=mesh['fsdp'=8,'rep'=4] {'fsdp'}, dimensions={0}, use_global_device_ids=true | all-gather | bytes 497664 | tf_op jit(solution)/shard_map/all_gather | solution.py:494
  511.9 1.8 fusion.75
  514.4 3.3 all-to-all-start.1
  517.8 1.6 convert_reduce_fusion
  519.5 45.2 %psum.43 = f32[4608]{0:T(1024)S(1)} all-reduce(f32[4608]{0:T(1024)S(1)} %pad_maximum_fusion.1), channel_id=1, replica_groups=mesh['fsdp'=8,'rep'=4] {'fsdp','rep'}, use_global_device_ids=true, to_apply=%region_20.21 | all-reduce | flops 4608 | bytes 36864 | tf_op jit(solution)/shard_map/psum | solution.py:502
  566.7 10.9 %psum.46 = f32[576]{0:T(1024)} all-reduce(f32[576]{0:T(1024)S(1)} %dynamic-slice_reduce_fusion), channel_id=1, replica_groups=mesh['fsdp'=8,'rep'=4] {'rep'}, use_global_device_ids=true, to_apply=%region_24.25 | all-reduce | flops 576 | bytes 4608 | tf_op jit(solution)/shard_map/psum | solution.py:506
  578.4 3.9 reshape.177
  582.3 1.9 convert_reduce_fusion.1
  584.9 3.6 fusion.42
  588.5 53.3 %all-reduce.8.cloned.1.call-done = (bf16[144,3456]{1,0:T(8,128)(2,1)}, bf16[144,1152]{1,0:T(8,128)(2,1)}, bf16[144,4608]{1,0:T(8,128)(2,1)}, bf16[576,1152]{1,0:T(8,128)(2,1)}) async-done(((bf16[144,3456]{1,0:T(8,128)(2,1)}, bf16[144,1152]{1,0:T(8,128)(2,1)}, bf16[144,4608]{1,0:T(8,128)(2,1)}, bf16[576,1152]{1,0:T(8,128)(2,1)}), (bf16[144,3456]{1,0:T(8,128)(2,1)}, bf16[144,1152]{1,0:T(8,128)(2,1)}, ...) | async-done | bytes 3981328 | tf_op jit(solution)/shard_map/psum | solution.py:518
  641.8 1.9 convert_element_type.116
  643.7 1.4 convert_element_type.111
  645.6 1.8 convert_element_type.118
  647.4 1.7 convert_element_type.119
  (196 shorter events, 35.9 us)
Async XLA Ops:
  7.2 11.7 %copy-start = (bf16[144,6912]{1,0:T(8,128)(2,1)S(1)}, bf16[144,6912]{1,0:T(8,128)(2,1)}, u32[]{:S(2)}) copy-start(bf16[144,6912]{1,0:T(8,128)(2,1)} %param.17) | copy-start | bytes 5971972
  7.2 75.0 %all-reduce.6.cloned.1.call-start = ((), (), s32[]{:S(2)}) async-start(), calls=%async_computation.10 | async-start | bytes 1769472
  20.3 115.6 %all-gather.9.cloned.1.call-start = ((), (), s32[]{:S(2)}) async-start(), calls=%async_computation.5 | async-start | bytes 8957952 | tf_op jit(solution)/shard_map/all_gather | solution.py:419
  27.1 5.3 copy-start.41
  27.1 6.6 copy-start.43
  27.1 6.6 %copy-start.44 = (bf16[288]{0:T(512)(128)(2,1)S(1)}, bf16[288]{0:T(512)(128)(2,1)}, u32[]{:S(2)}) copy-start(bf16[288]{0:T(512)(128)(2,1)} %param.20) | copy-start | bytes 1732
  27.1 6.6 %copy-start.45 = (bf16[144]{0:T(256)(128)(2,1)S(1)}, bf16[144]{0:T(256)(128)(2,1)}, u32[]{:S(2)}) copy-start(bf16[144]{0:T(256)(128)(2,1)} %param.22) | copy-start | bytes 868
  27.1 6.6 %copy-start.46 = (bf16[144]{0:T(256)(128)(2,1)S(1)}, bf16[144]{0:T(256)(128)(2,1)}, u32[]{:S(2)}) copy-start(bf16[144]{0:T(256)(128)(2,1)} %param.26) | copy-start | bytes 868
  27.1 43.5 %copy-start.42 = (bf16[576]{0:T(1024)(128)(2,1)S(1)}, bf16[576]{0:T(1024)(128)(2,1)}, u32[]{:S(2)}) copy-start(bf16[576]{0:T(1024)(128)(2,1)} %param.24) | copy-start | bytes 3460
  27.1 45.3 %copy-start.47 = (s32[4]{0:T(128)S(1)}, s32[4]{0:T(128)}, u32[]{:S(2)}) copy-start(s32[4]{0:T(128)} %param.16) | copy-start | bytes 52
  27.1 45.5 %copy-start.5 = (bf16[256,1152]{1,0:T(8,128)(2,1)S(1)}, bf16[256,1152]{1,0:T(8,128)(2,1)}, u32[]{:S(2)}) copy-start(bf16[256,1152]{1,0:T(8,128)(2,1)} %param.14) | copy-start | bytes 1769476
  27.1 149.8 %all-to-all-start = ((bf16[8,144,640]{2,1,0:T(8,128)(2,1)}), bf16[8,144,640]{2,1,0:T(8,128)(2,1)}, u32[]{:S(2)}, u32[]{:S(2)}) async-start(bf16[8,144,640]{2,1,0:T(8,128)(2,1)} %bitcast_dynamic-update-slice_fusion), calls=%async_computation | async-start | bytes 2949120 | tf_op jit(solution)/shard_map/all_to_all | solution.py:458
  31.6 136.5 %all-gather.11.cloned.1.call-start = ((), (), s32[]{:S(2)}) async-start(), calls=%async_computation.6 | async-start | bytes 2985984 | tf_op jit(solution)/shard_map/all_gather | solution.py:420
  32.3 325.3 %reduce-scatter.5.cloned.1.call-start = ((), (), s32[]{:S(2)}) async-start(), calls=%async_computation.8 | async-start | bytes 2985984 | tf_op jit(solution)/shard_map/reduce_scatter | solution.py:508
  72.4 2.1 copy-start.39
  72.6 1.8 copy-start.31
  86.1 2.9 copy-start.1
  89.4 52.3 %copy-start.21 = (bf16[256,1152]{1,0:T(8,128)(2,1)}, bf16[256,1152]{1,0:T(8,128)(2,1)S(1)}, u32[]{:S(2)}) copy-start(bf16[256,1152]{1,0:T(8,128)(2,1)S(1)} %fusion.16) | copy-start | bytes 1769476
  144.3 7.4 %copy-start.25 = (bf16[256,1152]{0,1:T(8,128)(2,1)}, bf16[256,1152]{0,1:T(8,128)(2,1)S(1)}, u32[]{:S(2)}) copy-start(bf16[256,1152]{0,1:T(8,128)(2,1)S(1)} %copy.60) | copy-start | bytes 1769476
  145.8 5.9 copy-start.27
  295.0 2.2 copy-start.2
  295.0 2.3 copy-start.16
  297.3 3.1 copy-start.10
  300.4 2.1 copy-start.7
  300.4 2.9 copy-start.19
  305.8 124.9 %reduce-scatter.3.cloned.1.call-start = ((), (), s32[]{:S(2)}) async-start(), calls=%async_computation.7 | async-start | bytes 8957952 | tf_op jit(solution)/shard_map/reduce_scatter | solution.py:507
  311.9 4.5 copy-start.20
  318.6 2.1 copy-start.12
  319.9 1.6 copy-start.22
  327.0 27.2 %all-to-all-start.2 = ((bf16[8,144,640]{2,1,0:T(8,128)(2,1)}), bf16[8,144,640]{2,1,0:T(8,128)(2,1)}, u32[]{:S(2)}, u32[]{:S(2)}) async-start(bf16[8,144,640]{2,1,0:T(8,128)(2,1)} %bitcast.99), calls=%async_computation.4 | async-start | bytes 2949120 | tf_op jit(solution)/shard_map/all_to_all | solution.py:509
  331.3 247.1 %all-gather.13.cloned.1.call-start = ((), (), s32[]{:S(2)}) async-start(), calls=%async_computation.9 | async-start | bytes 1824768 | tf_op jit(solution)/shard_map/all_gather | solution.py:490
  331.4 7.2 %copy-start.6 = (bf16[256,1152]{1,0:T(8,128)(2,1)S(1)}, bf16[256,1152]{1,0:T(8,128)(2,1)}, u32[]{:S(2)}) copy-start(bf16[256,1152]{1,0:T(8,128)(2,1)} %param.14) | copy-start | bytes 1769476
  338.5 2.1 copy-start.8
  338.5 2.1 copy-start.11
  338.6 2.2 copy-start.18
  343.6 3.3 copy-start.34
  346.9 294.9 %all-reduce.8.cloned.1.call-start = ((), (), s32[]{:S(2)}) async-start(), calls=%async_computation.11 | async-start | bytes 7962624 | tf_op jit(solution)/shard_map/psum | solution.py:518
  356.3 74.4 %copy-start.30 = (bf16[144,4608]{1,0:T(8,128)(2,1)}, bf16[144,4608]{1,0:T(8,128)(2,1)S(1)}, u32[]{:S(2)}) copy-start(bf16[144,4608]{1,0:T(8,128)(2,1)S(1)} %fusion.36) | copy-start | bytes 3981316
  430.7 70.3 %copy-start.37 = (bf16[1,4,6912]{2,1,0:T(4,128)(2,1)S(1)}, bf16[1,4,6912]{2,1,0:T(4,128)(2,1)}, u32[]{:S(2)}) copy-start(bf16[1,4,6912]{2,1,0:T(4,128)(2,1)} %fusion.1) | copy-start | bytes 165892
  511.9 5.9 copy-start.13
  511.9 5.9 copy-start.15
  513.8 52.9 %copy-start.40 = (f32[1,640]{1,0:T(1,128)S(1)}, f32[1,640]{1,0:T(1,128)}, u32[]{:S(2)}) copy-start(f32[1,640]{1,0:T(1,128)} %get-tuple-element.21) | copy-start | bytes 7684
  513.8 64.0 %copy-start.38 = (bf16[4,1152]{1,0:T(4,128)(2,1)S(1)}, bf16[4,1152]{1,0:T(4,128)(2,1)}, u32[]{:S(2)}) copy-start(bf16[4,1152]{1,0:T(4,128)(2,1)} %param.15) | copy-start | bytes 27652
  514.4 63.2 %all-to-all-start.1 = ((f32[8,4,144]{2,1,0:T(4,128)}), f32[8,4,144]{2,1,0:T(4,128)S(1)}, u32[]{:S(2)}, u32[]{:S(2)}) async-start(f32[8,4,144]{2,1,0:T(4,128)} %reshape.161), calls=%async_computation.1 | async-start | bytes 65536 | tf_op jit(solution)/shard_map/all_to_all | solution.py:496
  582.3 2.6 copy-start.4
  641.8 1.9 copy-start.35
  643.7 1.9 copy-start.33
  645.6 1.8 copy-start.32
  (10 other events, 11.0 us)
Sparse Core Ops, SparseCore 0:
  20.4 61.8 all-reduce.5
  84.1 51.7 all-gather.8
  137.8 30.2 all-gather.10
  305.9 51.7 reduce-scatter.4
  361.4 69.1 reduce-scatter.2
  433.4 55.7 all-gather.12
  492.4 149.3 all-reduce.7
